TPU v7x, 32 devices: a whole 2x2x4 slice. The times are simulated.
32 devices in a mesh: row: 4 (over y, x), col: 8 (over z, core).
Axes of the slice: x: 2, y: 2, z: 4, core: 2. Of those that a mesh axis runs over, the one named last changes fastest.
Arguments:
- pair_repr: bfloat16 [1024, 1024, 128], P('row', 'col'), may hold values from -6 to 6
- logit_cotangent: bfloat16 [1024, 1024, 128], P('row', 'col'), may hold values from -6 to 6
- pair_mask: int32 [1024, 1024], P('row', 'col'), may hold values 0 or 1
- single_repr: bfloat16 [1024, 384], P(('row', 'col')), may hold values from -6 to 6
- token_index: int32 [1024], replicated, may hold values from 0 to 2046, as said below
- pair_up: bfloat16 [128, 512], replicated, may hold values from -0.5 to 0.5
- pair_gate: bfloat16 [128, 512], replicated, may hold values from -0.5 to 0.5
- pair_down: bfloat16 [512, 128], replicated, may hold values from -0.25 to 0.25
- head_weight: bfloat16 [128, 128], replicated, may hold values from -0.5 to 0.5
- rel_table: bfloat16 [65, 128], replicated, may hold values from -3 to 3
- proj_row: bfloat16 [384, 128], replicated, may hold values from -0.3125 to 0.3125
- proj_col: bfloat16 [384, 128], replicated, may hold values from -0.3125 to 0.3125
- single_gate: bfloat16 [384, 1536], replicated, may hold values from -0.3125 to 0.3125
- single_up: bfloat16 [384, 1536], replicated, may hold values from -0.3125 to 0.3125
- single_down: bfloat16 [1536, 384], replicated, may hold values from -0.15625 to 0.15625
Outputs:
- pair_grad: bfloat16 [1024, 1024, 128], P('row', 'col')
- single_grad: bfloat16 [1024, 384], P(('row', 'col'))
- grad_pair_up: float32 [128, 512], replicated
- grad_pair_gate: float32 [128, 512], replicated
- grad_pair_down: float32 [512, 128], replicated
- grad_head: float32 [128, 128], replicated
- grad_rel: float32 [65, 128], replicated
- grad_proj_row: float32 [384, 128], replicated
- grad_proj_col: float32 [384, 128], replicated
- grad_single_gate: float32 [384, 1536], P(None, ('row', 'col'))
- grad_single_up: float32 [384, 1536], P(None, ('row', 'col'))
- grad_single_down: float32 [1536, 384], P(('row', 'col'))
Inputs may be any that keep to these rules, and one draw needn't show every extreme that they name: `token_index`: strictly increasing, entry 0 is 0, successive entries differ by 1 to 3, the last entry is 2046.
All inputs are finite; a program needn't handle non-finite values. No bound on the sum of `pair_mask` on one device may be relied on, other than what follows from the above.
Results may differ from a plain program's by a relative error of at most 0.018.
Values may be sent and summed in bfloat16 or wider, within the bound.
No kernel may reach another device: no remote copies, remote signals or barrier semaphores. Data moves between devices by JAX's collectives and lax.ppermute only.
A program may use at most 192 MiB of HBM per device.

v0:
```python
import jax
import jax.numpy as jnp
from jax import lax
from jax.sharding import PartitionSpec as P

norm_eps = 1e-05


def gated_parts(gate):
    sigma = jax.nn.sigmoid(gate)
    return (gate * sigma, sigma * (1.0 + gate * (1.0 - sigma)))


def product(matrix_a, matrix_b):
    return jnp.dot(matrix_a, matrix_b, preferred_element_type=jnp.float32)


def product_left(matrix_a, matrix_b):
    return lax.dot_general(
        matrix_a, matrix_b, (((0,), (0,)), ((), ())), preferred_element_type=jnp.float32
    )


def product_right(matrix_a, matrix_b):
    return lax.dot_general(
        matrix_a, matrix_b, (((1,), (1,)), ((), ())), preferred_element_type=jnp.float32
    )


def single_forward(single_repr, single_gate, single_up, single_down):
    source = single_repr.astype(jnp.float32)
    inverse_rms = lax.rsqrt(jnp.mean(source * source, axis=-1, keepdims=True) + norm_eps)
    normed = source * inverse_rms
    normed_bf = normed.astype(jnp.bfloat16)
    gate_pre = product(normed_bf, single_gate)
    up_pre = product(normed_bf, single_up)
    silu_value, silu_slope = gated_parts(gate_pre)
    hidden = (silu_value * up_pre).astype(jnp.bfloat16)
    updated = (source + product(hidden, single_down)).astype(jnp.bfloat16)
    return (normed, inverse_rms, normed_bf, up_pre, silu_value, silu_slope, hidden, updated)


def single_backward(grad_in, saved_state, single_gate, single_up, single_down):
    normed, inverse_rms, normed_bf, up_pre, silu_value, silu_slope, hidden, updated = saved_state
    grad_bf = grad_in.astype(jnp.bfloat16)
    grad_hidden = product_right(grad_bf, single_down)
    grad_up = (grad_hidden * silu_value).astype(jnp.bfloat16)
    grad_gate = (grad_hidden * up_pre * silu_slope).astype(jnp.bfloat16)
    grad_normed = product_right(grad_gate, single_gate) + product_right(grad_up, single_up)
    grad_source = grad_in + inverse_rms * (
        grad_normed - normed * jnp.mean(grad_normed * normed, axis=-1, keepdims=True)
    )
    return (grad_source, grad_bf, grad_gate, grad_up)


def local_weight_sums(normed_bf, grad_bf, grad_gate, grad_up, hidden):
    return jnp.stack(
        [
            product_left(normed_bf, grad_gate),
            product_left(normed_bf, grad_up),
            product_left(grad_bf, hidden),
        ],
        axis=0,
    )


def pair_block(
    pair_blk,
    cot_blk,
    mirror_blk,
    row_blk,
    col_blk,
    row_pos,
    col_pos,
    rel_table,
    up_gate,
    pair_down,
    head_weight,
):
    n_rows, n_cols, pair_width = pair_blk.shape
    bin_count = mirror_blk.shape[2]
    rel_count = rel_table.shape[0]
    rel_span = (rel_count - 1) // 2
    pair_count = n_rows * n_cols
    offset = jnp.clip(row_pos[:, None] - col_pos[None, :], -rel_span, rel_span) + rel_span
    one_hot = offset.reshape(pair_count, 1) == jnp.arange(rel_count, dtype=jnp.int32)[None, :]
    hot_table = one_hot.astype(jnp.bfloat16)
    pair_in = (
        pair_blk.astype(jnp.float32)
        + row_blk.astype(jnp.float32)[:, None, :]
        + col_blk.astype(jnp.float32)[None, :, :]
    )
    pair_in = pair_in.reshape(pair_count, pair_width) + product(hot_table, rel_table)
    centred = pair_in - jnp.mean(pair_in, axis=-1, keepdims=True)
    inv_std = lax.rsqrt(jnp.mean(centred * centred, axis=-1, keepdims=True) + norm_eps)
    normed = centred * inv_std
    normed_bf = normed.astype(jnp.bfloat16)
    hidden_width = up_gate.shape[1] // 2
    both_pre = product(normed_bf, up_gate)
    up_pre = both_pre[:, :hidden_width]
    gate_pre = both_pre[:, hidden_width:]
    silu_value, silu_slope = gated_parts(gate_pre)
    hidden = (silu_value * up_pre).astype(jnp.bfloat16)
    pair_out = (pair_in + product(hidden, pair_down)).astype(jnp.bfloat16)
    cot_flat = cot_blk.reshape(pair_count, 2 * bin_count)
    symmetric = (
        cot_flat[:, bin_count:].astype(jnp.float32)
        + mirror_blk.reshape(pair_count, bin_count).astype(jnp.float32)
    ).astype(jnp.bfloat16)
    head_cot = jnp.concatenate([cot_flat[:, :bin_count], symmetric], axis=1)
    grad_out = product_right(head_cot, head_weight)
    grad_out_bf = grad_out.astype(jnp.bfloat16)
    grad_hidden = product_right(grad_out_bf, pair_down)
    grad_both = jnp.concatenate(
        [
            (grad_hidden * silu_value).astype(jnp.bfloat16),
            (grad_hidden * up_pre * silu_slope).astype(jnp.bfloat16),
        ],
        axis=1,
    )
    grad_normed = product_right(grad_both, up_gate)
    grad_in = grad_out + inv_std * (
        grad_normed
        - jnp.mean(grad_normed, axis=-1, keepdims=True)
        - normed * jnp.mean(grad_normed * normed, axis=-1, keepdims=True)
    )
    head_sum = product_left(pair_out, head_cot)
    down_sum = product_left(hidden, grad_out_bf)
    up_gate_sum = product_left(normed_bf, grad_both)
    rel_sum = lax.dot_general(
        one_hot.astype(jnp.float32),
        grad_in,
        (((0,), (0,)), ((), ())),
        precision=lax.Precision.HIGHEST,
        preferred_element_type=jnp.float32,
    )
    grad_tile = grad_in.reshape(n_rows, n_cols, pair_width)
    return (
        grad_tile.astype(jnp.bfloat16),
        jnp.sum(grad_tile, axis=1),
        jnp.sum(grad_tile, axis=0),
        up_gate_sum,
        down_sum,
        head_sum,
        rel_sum,
    )


def local(
    pair_repr,
    logit_cotangent,
    pair_mask,
    single_repr,
    token_index,
    pair_up,
    pair_gate,
    pair_down,
    head_weight,
    rel_table,
    proj_row,
    proj_col,
    single_gate,
    single_up,
    single_down,
):
    n_row = lax.axis_size("row")
    n_col = lax.axis_size("col")
    row_index = lax.axis_index("row")
    col_index = lax.axis_index("col")
    joint_index = row_index * n_col + col_index
    tile_rows, tile_cols, pair_width = pair_repr.shape
    bin_count = logit_cotangent.shape[2] // 2
    strip_len = single_repr.shape[0]
    tokens_all = strip_len * n_row * n_col
    hidden_width = pair_up.shape[1]
    saved_state = single_forward(single_repr, single_gate, single_up, single_down)
    updated = saved_state[7]
    row_piece = product(updated, proj_row).astype(jnp.bfloat16)
    col_piece = product(updated, proj_col).astype(jnp.bfloat16)
    row_proj = lax.all_gather(row_piece, "col", axis=0, tiled=True)
    col_whole = lax.all_gather(col_piece, ("row", "col"), axis=0, tiled=True)
    col_proj = lax.dynamic_slice_in_dim(col_whole, col_index * tile_cols, tile_cols, 0)
    masked = logit_cotangent * pair_mask[:, :, None].astype(jnp.bfloat16)
    distance_part = masked[:, :, bin_count:].reshape(tile_rows, tile_cols * bin_count)
    strips = lax.all_to_all(distance_part, "col", split_axis=0, concat_axis=1, tiled=True)
    columns = lax.all_to_all(strips, ("row", "col"), split_axis=1, concat_axis=0, tiled=True)
    returned = lax.all_to_all(columns, "col", split_axis=0, concat_axis=1, tiled=True)
    mirrored = returned.reshape(tile_cols, tile_rows, bin_count).transpose(1, 0, 2)
    up_gate = jnp.concatenate([pair_up, pair_gate], axis=1)
    row_pos = lax.dynamic_slice_in_dim(token_index, row_index * tile_rows, tile_rows, 0)
    col_pos = lax.dynamic_slice_in_dim(token_index, col_index * tile_cols, tile_cols, 0)
    block_count = 4
    block_rows = tile_rows // block_count

    def block_step(running, inputs):
        pair_blk, cot_blk, mirror_blk, row_blk, pos_blk = inputs
        grad_blk, row_sum, col_sum, up_gate_sum, down_sum, head_sum, rel_sum = pair_block(
            pair_blk,
            cot_blk,
            mirror_blk,
            row_blk,
            col_proj,
            pos_blk,
            col_pos,
            rel_table,
            up_gate,
            pair_down,
            head_weight,
        )
        running = (
            running[0] + col_sum,
            running[1] + up_gate_sum,
            running[2] + down_sum,
            running[3] + head_sum,
            running[4] + rel_sum,
        )
        return (running, (grad_blk, row_sum))

    initial = (
        jnp.zeros((tile_cols, pair_width), jnp.float32),
        jnp.zeros(up_gate.shape, jnp.float32),
        jnp.zeros(pair_down.shape, jnp.float32),
        jnp.zeros(head_weight.shape, jnp.float32),
        jnp.zeros(rel_table.shape, jnp.float32),
    )
    sliced = (
        pair_repr.reshape(block_count, block_rows, tile_cols, pair_width),
        masked.reshape(block_count, block_rows, tile_cols, 2 * bin_count),
        mirrored.reshape(block_count, block_rows, tile_cols, bin_count),
        row_proj.reshape(block_count, block_rows, pair_width),
        row_pos.reshape(block_count, block_rows),
    )
    sums_out, blocks_out = lax.scan(block_step, initial, sliced)
    col_total, up_gate_sum, down_sum, head_sum, rel_sum = sums_out
    grad_blocks, row_sums = blocks_out
    pair_grad = grad_blocks.reshape(tile_rows, tile_cols, pair_width)
    row_tile = row_sums.reshape(tile_rows, pair_width)
    row_part = lax.psum_scatter(
        row_tile.astype(jnp.bfloat16), "col", scatter_dimension=0, tiled=True
    )
    col_summed = lax.psum(col_total.astype(jnp.bfloat16), "row")
    col_every = lax.all_gather(col_summed, "col", axis=0, tiled=True)
    col_bf = lax.dynamic_slice_in_dim(col_every, joint_index * strip_len, strip_len, 0)
    single_cot = product_right(row_part, proj_row) + product_right(col_bf, proj_col)
    prow_sum = product_left(updated, row_part)
    pcol_sum = product_left(updated, col_bf)
    grad_source, grad_bf, grad_gate, grad_up = single_backward(
        single_cot, saved_state, single_gate, single_up, single_down
    )
    normed_bf = saved_state[2]
    hidden = saved_state[6]
    stacked = local_weight_sums(normed_bf, grad_bf, grad_gate, grad_up, hidden)
    summed = lax.psum(stacked, ("row", "col"))
    share_len = summed.shape[2] // (n_row * n_col)
    own_share = lax.dynamic_slice_in_dim(summed, joint_index * share_len, share_len, 2)
    totals = lax.psum(
        (up_gate_sum, down_sum, head_sum, rel_sum, prow_sum, pcol_sum), ("row", "col")
    )
    grad_scale = 1.0 / tokens_all
    return (
        pair_grad,
        grad_source.astype(jnp.bfloat16),
        totals[0][:, :hidden_width] * grad_scale,
        totals[0][:, hidden_width:] * grad_scale,
        totals[1] * grad_scale,
        totals[2] * grad_scale,
        totals[3] * grad_scale,
        totals[4] * grad_scale,
        totals[5] * grad_scale,
        own_share[0] * grad_scale,
        own_share[1] * grad_scale,
        jnp.transpose(own_share[2]) * grad_scale,
    )


def solution(mesh):
    placed = (
        P("row", "col", None),
        P("row", "col", None),
        P("row", "col"),
        P(("row", "col"), None),
        P(),
        P(),
        P(),
        P(),
        P(),
        P(),
        P(),
        P(),
        P(),
        P(),
        P(),
    )
    return jax.shard_map(
        local,
        mesh=mesh,
        in_specs=placed,
        out_specs=(
            P("row", "col", None),
            P(("row", "col"), None),
            P(),
            P(),
            P(),
            P(),
            P(),
            P(),
            P(),
            P(None, ("row", "col")),
            P(None, ("row", "col")),
            P(("row", "col"), None),
        ),
        check_vma=False,
    )
```

profile of v0, /device:TPU:0, one launch (start us, length us, event | category | flops | bytes accessed | tf_op | source)
XLA Modules:
  0.0 1154.7 jit_solution(11379093476381169805)
XLA Ops:
  8.2 8.6 broadcast_multiply_fusion.3
  16.8 9.9 slice.44
  26.8 12.1 %all_to_all.36 = bf16[8,32,8192]{2,1,0:T(8,128)(2,1)} reshape(bf16[256,128,64]{2,1,0:T(8,128)(2,1)} %slice.44) | data formatting | bytes 8388608 | tf_op jit(solution)/shard_map/all_to_all | solution.py:185
  38.8 100.3 %all_to_all.48 = bf16[8,32,8192]{2,1,0:T(8,128)(2,1)S(1)} all-to-all(bf16[8,32,8192]{2,1,0:T(8,128)(2,1)} %all_to_all.36), channel_id=1, replica_groups=mesh['row'=4,'col'=8] {'col'}, dimensions={0} | all-to-all | bytes 8388608 | tf_op jit(solution)/shard_map/all_to_all | solution.py:185
  139.1 4.3 copy.44
  143.4 7.9 all_to_all.39
  151.4 4.5 copy.45
  155.8 98.3 %all_to_all.49 = bf16[32,32,2048]{2,0,1:T(8,128)(2,1)} all-to-all(bf16[32,32,2048]{2,0,1:T(8,128)(2,1)S(1)} %copy.45), channel_id=1, replica_groups=mesh['row'=4,'col'=8] {'row','col'}, dimensions={1} | all-to-all | bytes 8388608 | tf_op jit(solution)/shard_map/all_to_all | solution.py:186
  254.2 4.7 all-to-all-start.2
  265.2 94.8 %all_gather.9 = bf16[256,128]{1,0:T(8,128)(2,1)} all-gather(bf16[32,128]{1,0:T(8,128)(2,1)S(1)} %convolution_convert_fusion.1), channel_id=1, replica_groups=mesh['row'=4,'col'=8] {'col'}, dimensions={0}, use_global_device_ids=true | all-gather | bytes 73728 | tf_op jit(solution)/shard_map/all_gather | solution.py:180
  360.1 40.0 %all_gather.10 = bf16[1024,128]{1,0:T(8,128)(2,1)S(1)} all-gather(bf16[32,128]{1,0:T(8,128)(2,1)S(1)} %convolution_convert_fusion), channel_id=1, replica_groups=mesh['row'=4,'col'=8] {'row','col'}, dimensions={0}, use_global_device_ids=true | all-gather | bytes 270336 | tf_op jit(solution)/shard_map/all_gather | solution.py:181
  400.9 6.5 copy.46
  407.4 482.4 %while.23 = (s32[]{:T(128)}, f32[128,128]{1,0:T(8,128)}, f32[128,1024]{1,0:T(8,128)}, f32[512,128]{1,0:T(8,128)}, f32[128,128]{1,0:T(8,128)}, /*index=5*/f32[65,...) while((s32[]{:T(128)}, f32[128,128]{1,0:T(8,128)}, ...), condition=%wide.region_8.9_spmd.clone, body=%wide.region_1.8_spmd.clone.sunk | while | flops 11331420160 | bytes 375022848 | solution.py:233
  433.8 12.2 %fusion.127 = f32[8192,1024]{0,1:T(8,128)} fusion(bf16[128,1024]{1,0:T(8,128)(2,1)S(1)} %copy-done.9, f32[8192,128]{1,0:T(8,128)S(1)} %get-tuple-element.485, f32[8192]{0:T(1024)S(1)} %add_rsqrt_fusion.3, f32[8192]{0:T(1024)S(1)} %broadcast_multiply_fusion.13), kind=kOutput, calls=%fused_computation.53.clone.1 | convolution fusion | flops 2150629376 | bytes 38076416 | tf_op jit(solution)/shard_map/while/body/eval_jaxpr/dot_general | solution.py:15
  456.7 22.8 %multiply_convert_fusion.7 = (bf16[8192,512]{0,1:T(8,128)(2,1)}, bf16[8192,512]{0,1:T(8,128)(2,1)}, bf16[8192,512]{0,1:T(8,128)(2,1)}) fusion(f32[8192,1024]{0,1:T(8,128)} %fusion.127, bf16[512,128]{1,0:T(8,128)(2,1)S(1)} %get-tuple-element.556, f32[8192,128]{1,0:T(8,128)} %fusion.124), kind=kOutput, calls=%fused_computation.3.clone.1 | convolution fusion | flops 1137704960 | bytes 63045632 | tf_op jit(solution)/shard_map/while/body/eval_jaxpr/dot_general | solution.py:25
  479.4 13.2 %fusion.128 = (f32[8192]{0:T(1024)S(1)}, f32[8192]{0:T(1024)S(1)}, f32[8192,128]{1,0:T(8,128)S(1)}) fusion(f32[8192]{0:T(1024)S(1)} %add_rsqrt_fusion.3, f32[8192,128]{1,0:T(8,128)S(1)} %copy-done.2, f32[8192]{0:T(1024)S(1)} %broadcast_multiply_fusion.13, bf16[128,1024]{1,0:T(8,128)(2,1)S(1)} %copy-done.10, ...), kind=kOutput, calls=%fused_computation.108.clone.1 | convolution fusion | flops 2186264576 | bytes 25559040 | tf_op jit(solution)/shard_map/while/body/eval_jaxpr/dot_general | solution.py:25
  492.7 5.0 bitcast_reduce_fusion.2
  500.8 11.2 fusion.130
  512.1 7.8 convolution_add_fusion.7
  519.9 12.5 %fusion.129 = f32[128,1024]{1,0:T(8,128)S(1)} fusion(bf16[8192,512]{0,1:T(8,128)(2,1)} %get-tuple-element.487, bf16[8192,512]{0,1:T(8,128)(2,1)} %get-tuple-element.488, f32[128,1024]{1,0:T(8,128)S(1)} %copy-done.26, pred[]{:T(512)S(6)} %compare.3, f32[8192,128]{1,0:T(8,128)S(1)} %copy-done.3, f32[8192]{0:T(1024)S(1)} %add_rsqrt_fusion.3, ...), kind=kOutput, calls=%fused_computation.23.clone.1 | convolution fusion | flops 2184445952 | bytes 22085632 | tf_op jit(solution)/shard_map/while/body/eval_jaxpr/dot_general | solution.py:19
  535.1 4.2 fusion.131
  550.4 12.2 %fusion.127 = f32[8192,1024]{0,1:T(8,128)} fusion(bf16[128,1024]{1,0:T(8,128)(2,1)S(1)} %copy-done.9, f32[8192,128]{1,0:T(8,128)S(1)} %get-tuple-element.485, f32[8192]{0:T(1024)S(1)} %add_rsqrt_fusion.3, f32[8192]{0:T(1024)S(1)} %broadcast_multiply_fusion.13), kind=kOutput, calls=%fused_computation.53.clone.1 | convolution fusion | flops 2150629376 | bytes 38076416 | tf_op jit(solution)/shard_map/while/body/eval_jaxpr/dot_general | solution.py:15
  573.2 22.8 %multiply_convert_fusion.7 = (bf16[8192,512]{0,1:T(8,128)(2,1)}, bf16[8192,512]{0,1:T(8,128)(2,1)}, bf16[8192,512]{0,1:T(8,128)(2,1)}) fusion(f32[8192,1024]{0,1:T(8,128)} %fusion.127, bf16[512,128]{1,0:T(8,128)(2,1)S(1)} %get-tuple-element.556, f32[8192,128]{1,0:T(8,128)} %fusion.124), kind=kOutput, calls=%fused_computation.3.clone.1 | convolution fusion | flops 1137704960 | bytes 63045632 | tf_op jit(solution)/shard_map/while/body/eval_jaxpr/dot_general | solution.py:25
  596.0 13.2 %fusion.128 = (f32[8192]{0:T(1024)S(1)}, f32[8192]{0:T(1024)S(1)}, f32[8192,128]{1,0:T(8,128)S(1)}) fusion(f32[8192]{0:T(1024)S(1)} %add_rsqrt_fusion.3, f32[8192,128]{1,0:T(8,128)S(1)} %copy-done.2, f32[8192]{0:T(1024)S(1)} %broadcast_multiply_fusion.13, bf16[128,1024]{1,0:T(8,128)(2,1)S(1)} %copy-done.10, ...), kind=kOutput, calls=%fused_computation.108.clone.1 | convolution fusion | flops 2186264576 | bytes 25559040 | tf_op jit(solution)/shard_map/while/body/eval_jaxpr/dot_general | solution.py:25
  609.3 5.0 bitcast_reduce_fusion.2
  617.4 11.2 fusion.130
  628.6 7.8 convolution_add_fusion.7
  636.4 12.5 %fusion.129 = f32[128,1024]{1,0:T(8,128)S(1)} fusion(bf16[8192,512]{0,1:T(8,128)(2,1)} %get-tuple-element.487, bf16[8192,512]{0,1:T(8,128)(2,1)} %get-tuple-element.488, f32[128,1024]{1,0:T(8,128)S(1)} %copy-done.26, pred[]{:T(512)S(6)} %compare.3, f32[8192,128]{1,0:T(8,128)S(1)} %copy-done.3, f32[8192]{0:T(1024)S(1)} %add_rsqrt_fusion.3, ...), kind=kOutput, calls=%fused_computation.23.clone.1 | convolution fusion | flops 2184445952 | bytes 22085632 | tf_op jit(solution)/shard_map/while/body/eval_jaxpr/dot_general | solution.py:19
  666.9 12.2 %fusion.127 = f32[8192,1024]{0,1:T(8,128)} fusion(bf16[128,1024]{1,0:T(8,128)(2,1)S(1)} %copy-done.9, f32[8192,128]{1,0:T(8,128)S(1)} %get-tuple-element.485, f32[8192]{0:T(1024)S(1)} %add_rsqrt_fusion.3, f32[8192]{0:T(1024)S(1)} %broadcast_multiply_fusion.13), kind=kOutput, calls=%fused_computation.53.clone.1 | convolution fusion | flops 2150629376 | bytes 38076416 | tf_op jit(solution)/shard_map/while/body/eval_jaxpr/dot_general | solution.py:15
  689.8 22.8 %multiply_convert_fusion.7 = (bf16[8192,512]{0,1:T(8,128)(2,1)}, bf16[8192,512]{0,1:T(8,128)(2,1)}, bf16[8192,512]{0,1:T(8,128)(2,1)}) fusion(f32[8192,1024]{0,1:T(8,128)} %fusion.127, bf16[512,128]{1,0:T(8,128)(2,1)S(1)} %get-tuple-element.556, f32[8192,128]{1,0:T(8,128)} %fusion.124), kind=kOutput, calls=%fused_computation.3.clone.1 | convolution fusion | flops 1137704960 | bytes 63045632 | tf_op jit(solution)/shard_map/while/body/eval_jaxpr/dot_general | solution.py:25
  712.5 13.2 %fusion.128 = (f32[8192]{0:T(1024)S(1)}, f32[8192]{0:T(1024)S(1)}, f32[8192,128]{1,0:T(8,128)S(1)}) fusion(f32[8192]{0:T(1024)S(1)} %add_rsqrt_fusion.3, f32[8192,128]{1,0:T(8,128)S(1)} %copy-done.2, f32[8192]{0:T(1024)S(1)} %broadcast_multiply_fusion.13, bf16[128,1024]{1,0:T(8,128)(2,1)S(1)} %copy-done.10, ...), kind=kOutput, calls=%fused_computation.108.clone.1 | convolution fusion | flops 2186264576 | bytes 25559040 | tf_op jit(solution)/shard_map/while/body/eval_jaxpr/dot_general | solution.py:25
  725.8 5.0 bitcast_reduce_fusion.2
  733.9 11.2 fusion.130
  745.2 7.8 convolution_add_fusion.7
  753.0 12.5 %fusion.129 = f32[128,1024]{1,0:T(8,128)S(1)} fusion(bf16[8192,512]{0,1:T(8,128)(2,1)} %get-tuple-element.487, bf16[8192,512]{0,1:T(8,128)(2,1)} %get-tuple-element.488, f32[128,1024]{1,0:T(8,128)S(1)} %copy-done.26, pred[]{:T(512)S(6)} %compare.3, f32[8192,128]{1,0:T(8,128)S(1)} %copy-done.3, f32[8192]{0:T(1024)S(1)} %add_rsqrt_fusion.3, ...), kind=kOutput, calls=%fused_computation.23.clone.1 | convolution fusion | flops 2184445952 | bytes 22085632 | tf_op jit(solution)/shard_map/while/body/eval_jaxpr/dot_general | solution.py:19
  768.2 4.2 fusion.131
  783.5 12.2 %fusion.127 = f32[8192,1024]{0,1:T(8,128)} fusion(bf16[128,1024]{1,0:T(8,128)(2,1)S(1)} %copy-done.9, f32[8192,128]{1,0:T(8,128)S(1)} %get-tuple-element.485, f32[8192]{0:T(1024)S(1)} %add_rsqrt_fusion.3, f32[8192]{0:T(1024)S(1)} %broadcast_multiply_fusion.13), kind=kOutput, calls=%fused_computation.53.clone.1 | convolution fusion | flops 2150629376 | bytes 38076416 | tf_op jit(solution)/shard_map/while/body/eval_jaxpr/dot_general | solution.py:15
  806.3 22.8 %multiply_convert_fusion.7 = (bf16[8192,512]{0,1:T(8,128)(2,1)}, bf16[8192,512]{0,1:T(8,128)(2,1)}, bf16[8192,512]{0,1:T(8,128)(2,1)}) fusion(f32[8192,1024]{0,1:T(8,128)} %fusion.127, bf16[512,128]{1,0:T(8,128)(2,1)S(1)} %get-tuple-element.556, f32[8192,128]{1,0:T(8,128)} %fusion.124), kind=kOutput, calls=%fused_computation.3.clone.1 | convolution fusion | flops 1137704960 | bytes 63045632 | tf_op jit(solution)/shard_map/while/body/eval_jaxpr/dot_general | solution.py:25
  829.1 13.2 %fusion.128 = (f32[8192]{0:T(1024)S(1)}, f32[8192]{0:T(1024)S(1)}, f32[8192,128]{1,0:T(8,128)S(1)}) fusion(f32[8192]{0:T(1024)S(1)} %add_rsqrt_fusion.3, f32[8192,128]{1,0:T(8,128)S(1)} %copy-done.2, f32[8192]{0:T(1024)S(1)} %broadcast_multiply_fusion.13, bf16[128,1024]{1,0:T(8,128)(2,1)S(1)} %copy-done.10, ...), kind=kOutput, calls=%fused_computation.108.clone.1 | convolution fusion | flops 2186264576 | bytes 25559040 | tf_op jit(solution)/shard_map/while/body/eval_jaxpr/dot_general | solution.py:25
  842.3 5.0 bitcast_reduce_fusion.2
  850.5 11.2 fusion.130
  861.7 7.8 convolution_add_fusion.7
  869.5 12.5 %fusion.129 = f32[128,1024]{1,0:T(8,128)S(1)} fusion(bf16[8192,512]{0,1:T(8,128)(2,1)} %get-tuple-element.487, bf16[8192,512]{0,1:T(8,128)(2,1)} %get-tuple-element.488, f32[128,1024]{1,0:T(8,128)S(1)} %copy-done.26, pred[]{:T(512)S(6)} %compare.3, f32[8192,128]{1,0:T(8,128)S(1)} %copy-done.3, f32[8192]{0:T(1024)S(1)} %add_rsqrt_fusion.3, ...), kind=kOutput, calls=%fused_computation.23.clone.1 | convolution fusion | flops 2184445952 | bytes 22085632 | tf_op jit(solution)/shard_map/while/body/eval_jaxpr/dot_general | solution.py:19
  890.7 14.0 %psum.56 = bf16[128,128]{1,0:T(8,128)(2,1)S(1)} all-reduce(bf16[128,128]{1,0:T(8,128)(2,1)S(1)} %convert_element_type.121), channel_id=1, replica_groups=mesh['row'=4,'col'=8] {'row'}, use_global_device_ids=true, to_apply=%region_10.11 | all-reduce | flops 16384 | bytes 65536 | tf_op jit(solution)/shard_map/psum | solution.py:241
  904.6 14.2 %all_gather.11 = bf16[1024,128]{1,0:T(8,128)(2,1)S(1)} all-gather(bf16[128,128]{1,0:T(8,128)(2,1)S(1)} %psum.56), channel_id=1, replica_groups=mesh['row'=4,'col'=8] {'col'}, dimensions={0}, use_global_device_ids=true | all-gather | bytes 294912 | tf_op jit(solution)/shard_map/all_gather | solution.py:242
  920.5 26.6 %reduce-scatter.2.cloned.1.call-done = bf16[32,128]{1,0:T(8,128)(2,1)} async-done(((bf16[256,128]{1,0:T(8,128)(2,1)}), bf16[32,128]{1,0:T(8,128)(2,1)}) %reduce-scatter.2.cloned.1.call-update) | async-done | bytes 8208 | tf_op jit(solution)/shard_map/reduce_scatter | solution.py:238
  958.8 40.0 %psum.60 = f32[65,128]{1,0:T(8,128)S(1)} all-reduce(f32[65,128]{1,0:T(8,128)S(1)} %copy-done.20), channel_id=1, replica_groups=mesh['row'=4,'col'=8] {'row','col'}, use_global_device_ids=true, to_apply=%region_15.16 | all-reduce | flops 8320 | bytes 66560 | tf_op jit(solution)/shard_map/psum | solution.py:256
  1001.2 135.8 %all-reduce.3.cloned.1.call-done = (f32[128,1024]{1,0:T(8,128)}, f32[512,128]{1,0:T(8,128)}, f32[128,128]{1,0:T(8,128)}, f32[384,128]{1,0:T(8,128)}, f32[384,128]{1,0:T(8,128)}, /*index=5*/f32[3,384,1536]{2,1,0:T(8,128)}) async-done(((f32[128,1024]{1,0:T(8,128)}, f32[512,128]{1,0:T(8,128)}, f32[128,128]{1,0:T(8,128)}, f32[384,128]{1,0:T(8,128)}, f32[384,128]{1,0:T(8,128)}, ...) | async-done | bytes 8323088 | tf_op jit(solution)/shard_map/psum | solution.py:256
  (314 shorter events, 152.7 us)
Async XLA Ops:
  7.2 255.2 %copy-start = (bf16[384,1536]{1,0:T(8,128)(2,1)S(1)}, bf16[384,1536]{1,0:T(8,128)(2,1)}, u32[]{:S(2)}) copy-start(bf16[384,1536]{1,0:T(8,128)(2,1)} %param.30) | copy-start | bytes 3538948
  254.2 7.7 copy-start.16
  254.2 7.8 copy-start.11
  254.2 146.7 %all-to-all-start.2 = ((bf16[8,128,2048]{2,1,0:T(8,128)(2,1)}), bf16[8,128,2048]{2,1,0:T(8,128)(2,1)}, u32[]{:S(2)}, u32[]{:S(2)}) async-start(bf16[8,128,2048]{2,1,0:T(8,128)(2,1)} %bitcast.135), calls=%async_computation.2 | async-start | bytes 8388608 | tf_op jit(solution)/shard_map/all_to_all | solution.py:187
  258.9 101.1 %copy-start.30 = (bf16[384,128]{1,0:T(8,128)(2,1)S(1)}, bf16[384,128]{1,0:T(8,128)(2,1)}, u32[]{:S(2)}) copy-start(bf16[384,128]{1,0:T(8,128)(2,1)} %param.28) | copy-start | bytes 294916
  258.9 141.3 %copy-start.31 = (bf16[128,512]{1,0:T(8,128)(2,1)S(1)}, bf16[128,512]{1,0:T(8,128)(2,1)}, u32[]{:S(2)}) copy-start(bf16[128,512]{1,0:T(8,128)(2,1)} %param.23) | copy-start | bytes 393220
  258.9 141.3 %copy-start.32 = (bf16[128,512]{1,0:T(8,128)(2,1)S(1)}, bf16[128,512]{1,0:T(8,128)(2,1)}, u32[]{:S(2)}) copy-start(bf16[128,512]{1,0:T(8,128)(2,1)} %param.22) | copy-start | bytes 393220
  258.9 688.2 %reduce-scatter.2.cloned.1.call-start = ((), (), s32[]{:S(2)}) async-start(), calls=%async_computation.4 | async-start | bytes 73728 | tf_op jit(solution)/shard_map/reduce_scatter | solution.py:238
  262.3 137.8 %copy-start.23 = (f32[32,1536]{1,0:T(8,128)}, f32[32,1536]{1,0:T(8,128)S(1)}, u32[]{:S(2)}) copy-start(f32[32,1536]{1,0:T(8,128)S(1)} %fusion.52) | copy-start | bytes 589828
  263.4 96.7 %copy-start.21 = (bf16[32,1536]{1,0:T(8,128)(2,1)}, bf16[32,1536]{1,0:T(8,128)(2,1)S(1)}, u32[]{:S(2)}) copy-start(bf16[32,1536]{1,0:T(8,128)(2,1)S(1)} %get-tuple-element.350) | copy-start | bytes 294916
  265.0 135.1 %copy-start.24 = (bf16[32,384]{1,0:T(8,128)(2,1)}, bf16[32,384]{1,0:T(8,128)(2,1)S(1)}, u32[]{:S(2)}) copy-start(bf16[32,384]{1,0:T(8,128)(2,1)S(1)} %fusion.26) | copy-start | bytes 73732
  400.9 6.5 copy-start.13
  425.9 27.5 %copy-start.6 = (bf16[1,64,128,128]{3,2,1,0:T(8,128)(2,1)}, bf16[1,64,128,128]{3,2,1,0:T(8,128)(2,1)S(1)}, u32[]{:S(2)}) copy-start(bf16[1,64,128,128]{3,2,1,0:T(8,128)(2,1)S(1)} %get-tuple-element.483) | copy-start | bytes 6291460 | tf_op jit(solution)/shard_map/while
  431.3 14.7 %copy-start.1 = (f32[8192,128]{1,0:T(8,128)}, f32[8192,128]{1,0:T(8,128)S(1)}, u32[]{:S(2)}) copy-start(f32[8192,128]{1,0:T(8,128)S(1)} %get-tuple-element.485) | copy-start | bytes 12582916 | tf_op jit(solution)/shard_map/while
  456.7 22.8 %copy-start.2 = (f32[8192,128]{1,0:T(8,128)S(1)}, f32[8192,128]{1,0:T(8,128)}, u32[]{:S(2)}) copy-start(f32[8192,128]{1,0:T(8,128)} %copy-done.1) | copy-start | bytes 12582916 | tf_op jit(solution)/shard_map/while
  456.7 22.8 %copy-start.10 = (bf16[128,1024]{1,0:T(8,128)(2,1)S(1)}, bf16[128,1024]{1,0:T(8,128)(2,1)}, u32[]{:S(2)}) copy-start(bf16[128,1024]{1,0:T(8,128)(2,1)} %get-tuple-element.557) | copy-start | bytes 786436 | tf_op jit(solution)/shard_map/while
  479.4 13.3 %copy-start.5 = (f32[8192,128]{1,0:T(8,128)S(1)}, f32[8192,128]{1,0:T(8,128)}, u32[]{:S(2)}) copy-start(f32[8192,128]{1,0:T(8,128)} %fusion.124) | copy-start | bytes 12582916 | tf_op jit(solution)/shard_map/while
  512.1 7.8 copy-start.3
  512.1 7.8 copy-start.26
  532.4 6.9 copy-start.27
  542.5 27.5 %copy-start.6 = (bf16[1,64,128,128]{3,2,1,0:T(8,128)(2,1)}, bf16[1,64,128,128]{3,2,1,0:T(8,128)(2,1)S(1)}, u32[]{:S(2)}) copy-start(bf16[1,64,128,128]{3,2,1,0:T(8,128)(2,1)S(1)} %get-tuple-element.483) | copy-start | bytes 6291460 | tf_op jit(solution)/shard_map/while
  547.8 14.7 %copy-start.1 = (f32[8192,128]{1,0:T(8,128)}, f32[8192,128]{1,0:T(8,128)S(1)}, u32[]{:S(2)}) copy-start(f32[8192,128]{1,0:T(8,128)S(1)} %get-tuple-element.485) | copy-start | bytes 12582916 | tf_op jit(solution)/shard_map/while
  573.2 22.8 %copy-start.2 = (f32[8192,128]{1,0:T(8,128)S(1)}, f32[8192,128]{1,0:T(8,128)}, u32[]{:S(2)}) copy-start(f32[8192,128]{1,0:T(8,128)} %copy-done.1) | copy-start | bytes 12582916 | tf_op jit(solution)/shard_map/while
  573.2 22.8 %copy-start.10 = (bf16[128,1024]{1,0:T(8,128)(2,1)S(1)}, bf16[128,1024]{1,0:T(8,128)(2,1)}, u32[]{:S(2)}) copy-start(bf16[128,1024]{1,0:T(8,128)(2,1)} %get-tuple-element.557) | copy-start | bytes 786436 | tf_op jit(solution)/shard_map/while
  596.0 13.3 %copy-start.5 = (f32[8192,128]{1,0:T(8,128)S(1)}, f32[8192,128]{1,0:T(8,128)}, u32[]{:S(2)}) copy-start(f32[8192,128]{1,0:T(8,128)} %fusion.124) | copy-start | bytes 12582916 | tf_op jit(solution)/shard_map/while
  628.6 7.8 copy-start.3
  628.6 7.8 copy-start.26
  649.0 6.9 copy-start.27
  659.0 27.5 %copy-start.6 = (bf16[1,64,128,128]{3,2,1,0:T(8,128)(2,1)}, bf16[1,64,128,128]{3,2,1,0:T(8,128)(2,1)S(1)}, u32[]{:S(2)}) copy-start(bf16[1,64,128,128]{3,2,1,0:T(8,128)(2,1)S(1)} %get-tuple-element.483) | copy-start | bytes 6291460 | tf_op jit(solution)/shard_map/while
  664.4 14.7 %copy-start.1 = (f32[8192,128]{1,0:T(8,128)}, f32[8192,128]{1,0:T(8,128)S(1)}, u32[]{:S(2)}) copy-start(f32[8192,128]{1,0:T(8,128)S(1)} %get-tuple-element.485) | copy-start | bytes 12582916 | tf_op jit(solution)/shard_map/while
  689.8 22.8 %copy-start.2 = (f32[8192,128]{1,0:T(8,128)S(1)}, f32[8192,128]{1,0:T(8,128)}, u32[]{:S(2)}) copy-start(f32[8192,128]{1,0:T(8,128)} %copy-done.1) | copy-start | bytes 12582916 | tf_op jit(solution)/shard_map/while
  689.8 22.8 %copy-start.10 = (bf16[128,1024]{1,0:T(8,128)(2,1)S(1)}, bf16[128,1024]{1,0:T(8,128)(2,1)}, u32[]{:S(2)}) copy-start(bf16[128,1024]{1,0:T(8,128)(2,1)} %get-tuple-element.557) | copy-start | bytes 786436 | tf_op jit(solution)/shard_map/while
  712.5 13.3 %copy-start.5 = (f32[8192,128]{1,0:T(8,128)S(1)}, f32[8192,128]{1,0:T(8,128)}, u32[]{:S(2)}) copy-start(f32[8192,128]{1,0:T(8,128)} %fusion.124) | copy-start | bytes 12582916 | tf_op jit(solution)/shard_map/while
  745.2 7.8 copy-start.3
  745.2 7.8 copy-start.26
  765.5 6.9 copy-start.27
  775.6 27.5 %copy-start.6 = (bf16[1,64,128,128]{3,2,1,0:T(8,128)(2,1)}, bf16[1,64,128,128]{3,2,1,0:T(8,128)(2,1)S(1)}, u32[]{:S(2)}) copy-start(bf16[1,64,128,128]{3,2,1,0:T(8,128)(2,1)S(1)} %get-tuple-element.483) | copy-start | bytes 6291460 | tf_op jit(solution)/shard_map/while
  780.9 14.7 %copy-start.1 = (f32[8192,128]{1,0:T(8,128)}, f32[8192,128]{1,0:T(8,128)S(1)}, u32[]{:S(2)}) copy-start(f32[8192,128]{1,0:T(8,128)S(1)} %get-tuple-element.485) | copy-start | bytes 12582916 | tf_op jit(solution)/shard_map/while
  806.3 22.8 %copy-start.2 = (f32[8192,128]{1,0:T(8,128)S(1)}, f32[8192,128]{1,0:T(8,128)}, u32[]{:S(2)}) copy-start(f32[8192,128]{1,0:T(8,128)} %copy-done.1) | copy-start | bytes 12582916 | tf_op jit(solution)/shard_map/while
  806.3 22.8 %copy-start.10 = (bf16[128,1024]{1,0:T(8,128)(2,1)S(1)}, bf16[128,1024]{1,0:T(8,128)(2,1)}, u32[]{:S(2)}) copy-start(bf16[128,1024]{1,0:T(8,128)(2,1)} %get-tuple-element.557) | copy-start | bytes 786436 | tf_op jit(solution)/shard_map/while
  829.1 13.3 %copy-start.5 = (f32[8192,128]{1,0:T(8,128)S(1)}, f32[8192,128]{1,0:T(8,128)}, u32[]{:S(2)}) copy-start(f32[8192,128]{1,0:T(8,128)} %fusion.124) | copy-start | bytes 12582916 | tf_op jit(solution)/shard_map/while
  861.7 7.8 copy-start.3
  861.7 7.8 copy-start.26
  882.1 6.9 copy-start.27
  889.8 62.7 %copy-start.17 = (bf16[32,384]{1,0:T(8,128)(2,1)S(1)}, bf16[32,384]{1,0:T(8,128)(2,1)}, u32[]{:S(2)}) copy-start(bf16[32,384]{1,0:T(8,128)(2,1)} %param.20) | copy-start | bytes 73732
  889.8 62.7 %copy-start.35 = (f32[32]{0:T(128)S(1)}, f32[32]{0:T(128)}, u32[]{:S(2)}) copy-start(f32[32]{0:T(128)} %copy-done.34) | copy-start | bytes 388
  918.9 218.1 %all-reduce.3.cloned.1.call-start = ((), (), s32[]{:S(2)}) async-start(), calls=%async_computation.5 | async-start | bytes 16646144 | tf_op jit(solution)/shard_map/psum | solution.py:256
  958.0 41.4 %copy-start.12 = (bf16[384,1536]{1,0:T(8,128)(2,1)S(1)}, bf16[384,1536]{1,0:T(8,128)(2,1)}, u32[]{:S(2)}) copy-start(bf16[384,1536]{1,0:T(8,128)(2,1)} %param.29) | copy-start | bytes 3538948
  (45 other events, 117.8 us)
Sparse Core Ops, SparseCore 0:
  919.0 28.1 reduce-scatter.1
  958.1 178.7 all-reduce.2
where the time goes:
time: 1170 us; the launch traced here: 1150 us
  blocking collectives  402 us (34%)
  matrix products  371 us (32%)
  waiting for transfers between devices  162 us (14%)
  local copies, waits for them, and re-layouts  102 us (9%)
  other arithmetic  81.1 us (7%)
  loops' own time  17.3 us (1%)
  between operations  14.7 us (1%)
    dot_general x17, matrix products, product_right(): lax.dot_general(matrix_a, matrix_b, (((1,), (1,)), ((), ())), preferred_e...  162 us
    psum x1, waiting for transfers between devices, local(): lax.psum((up_gate_sum, down_sum, head_sum, rel_sum, prow_sum, pcol_sum),...  136 us
    dot_general x17, matrix products, product_left(): lax.dot_general(matrix_a, matrix_b, (((0,), (0,)), ((), ())), preferred_e...  131 us
    all_to_all x1, blocking collectives, local(): lax.all_to_all(distance_part, 'col', split_axis=0, concat_axis=1, tiled=T...  100 us
    all_to_all x1, blocking collectives, local(): lax.all_to_all(strips, ('row', 'col'), split_axis=1, concat_axis=0, tiled...  98.3 us
    all_gather x1, blocking collectives, local(): row_proj = lax.all_gather(row_piece, 'col', axis=0, tiled=True)  94.8 us
    dot_general x13, matrix products, product(): return jnp.dot(matrix_a, matrix_b, preferred_element_type=jnp.float32)  61.4 us
    all_gather x1, blocking collectives, local(): col_whole = lax.all_gather(col_piece, ('row', 'col'), axis=0, tiled=True)  40 us
  transfers between devices with their start and end apart: 3, of which 2 were waited for; matrix products, arithmetic and copies ran while one was open for 1% of the time, Pallas kernels for 0%

commit v1 on v0

--- a/solution.py
+++ b/solution.py
@@ -254,7 +254,7 @@
     share_len = summed.shape[2] // (n_row * n_col)
     own_share = lax.dynamic_slice_in_dim(summed, joint_index * share_len, share_len, 2)
     totals = lax.psum(
-        (up_gate_sum, down_sum, head_sum, rel_sum, prow_sum, pcol_sum), ("row", "col")
+        lax.psum((up_gate_sum, down_sum, head_sum, rel_sum, prow_sum, pcol_sum), "row"), "col"
     )
     grad_scale = 1.0 / tokens_all
     return (

time: 1170 us -> 1260 us (1.077)
  waiting for transfers between devices: 162 us -> 251 us
    psum x0 -> x2, waiting for transfers between devices: none -> 174 us  [the longest x1 162 us: local(): summed = lax.psum(stacked, ('row', 'col'))]
    psum x1, waiting for transfers between devices: 136 us -> 50.2 us  [local(): lax.psum((up_gate_sum, down_sum, head_sum, rel_sum, prow_sum, pcol_sum),...]
    psum x0 -> x1, blocking collectives: none -> 26.6 us  [local(): lax.psum(lax.psum((up_gate_sum, down_sum, head_sum, rel_sum, prow_sum, pc...]
    psum x1, blocking collectives: 40 us -> 15.7 us  [local(): lax.psum((up_gate_sum, down_sum, head_sum, rel_sum, prow_sum, pcol_sum),...]
  transfers between devices with their start and end apart: 3 -> 5, of which waited for: 2 -> 4; matrix products, arithmetic and copies ran while one was open for 1% -> 2% of each run, Pallas kernels for 0% -> 0%
where the time goes in v1:
time: 1260 us; the launch traced here: 1250 us
  blocking collectives  404 us (32%)
  matrix products  374 us (30%)
  waiting for transfers between devices  251 us (20%)
  local copies, waits for them, and re-layouts  102 us (8%)
  other arithmetic  80.9 us (6%)
  loops' own time  17.3 us (1%)
  between operations  14.5 us (1%)
    dot_general x17, matrix products, product_right(): lax.dot_general(matrix_a, matrix_b, (((1,), (1,)), ((), ())), preferred_e...  162 us
    psum x1, waiting for transfers between devices, local(): summed = lax.psum(stacked, ('row', 'col'))  162 us
    dot_general x17, matrix products, product_left(): lax.dot_general(matrix_a, matrix_b, (((0,), (0,)), ((), ())), preferred_e...  134 us
    all_to_all x1, blocking collectives, local(): lax.all_to_all(distance_part, 'col', split_axis=0, concat_axis=1, tiled=T...  100 us
    all_to_all x1, blocking collectives, local(): lax.all_to_all(strips, ('row', 'col'), split_axis=1, concat_axis=0, tiled...  98.3 us
    all_gather x1, blocking collectives, local(): row_proj = lax.all_gather(row_piece, 'col', axis=0, tiled=True)  94.9 us
    dot_general x13, matrix products, product(): return jnp.dot(matrix_a, matrix_b, preferred_element_type=jnp.float32)  61.3 us
    psum x1, waiting for transfers between devices, local(): lax.psum((up_gate_sum, down_sum, head_sum, rel_sum, prow_sum, pcol_sum),...  50.2 us
  transfers between devices with their start and end apart: 5, of which 4 were waited for; matrix products, arithmetic and copies ran while one was open for 2% of the time, Pallas kernels for 0%

profile of v1, /device:TPU:0, one launch (start us, length us, event | category | flops | bytes accessed | tf_op | source)
XLA Modules:
  0.0 1248.6 jit_solution(8751020180651995329)
XLA Ops:
  8.2 8.6 broadcast_multiply_fusion.3
  16.8 9.9 slice.44
  26.8 12.0 all_to_all.36
  38.8 100.3 %all_to_all.48 = bf16[8,32,8192]{2,1,0:T(8,128)(2,1)S(1)} all-to-all(bf16[8,32,8192]{2,1,0:T(8,128)(2,1)} %all_to_all.36), channel_id=1, replica_groups=mesh['row'=4,'col'=8] {'col'}, dimensions={0} | all-to-all | bytes 8388608 | tf_op jit(solution)/shard_map/all_to_all | solution.py:185
  143.4 7.9 all_to_all.39
  151.3 4.5 copy.45
  155.8 98.3 %all_to_all.49 = bf16[32,32,2048]{2,0,1:T(8,128)(2,1)} all-to-all(bf16[32,32,2048]{2,0,1:T(8,128)(2,1)S(1)} %copy.45), channel_id=1, replica_groups=mesh['row'=4,'col'=8] {'row','col'}, dimensions={1} | all-to-all | bytes 8388608 | tf_op jit(solution)/shard_map/all_to_all | solution.py:186
  254.2 4.7 all-to-all-start.2
  265.1 94.9 %all_gather.9 = bf16[256,128]{1,0:T(8,128)(2,1)} all-gather(bf16[32,128]{1,0:T(8,128)(2,1)S(1)} %convolution_convert_fusion.1), channel_id=1, replica_groups=mesh['row'=4,'col'=8] {'col'}, dimensions={0}, use_global_device_ids=true | all-gather | bytes 73728 | tf_op jit(solution)/shard_map/all_gather | solution.py:180
  360.1 39.9 %all_gather.10 = bf16[1024,128]{1,0:T(8,128)(2,1)S(1)} all-gather(bf16[32,128]{1,0:T(8,128)(2,1)S(1)} %convolution_convert_fusion), channel_id=1, replica_groups=mesh['row'=4,'col'=8] {'row','col'}, dimensions={0}, use_global_device_ids=true | all-gather | bytes 270336 | tf_op jit(solution)/shard_map/all_gather | solution.py:181
  400.8 6.5 copy.46
  407.3 482.2 %while.23 = (s32[]{:T(128)}, f32[128,128]{1,0:T(8,128)}, f32[128,1024]{1,0:T(8,128)}, f32[512,128]{1,0:T(8,128)}, f32[128,128]{1,0:T(8,128)}, /*index=5*/f32[65,...) while((s32[]{:T(128)}, f32[128,128]{1,0:T(8,128)}, ...), condition=%wide.region_8.9_spmd.clone, body=%wide.region_1.8_spmd.clone.sunk | while | flops 11331420160 | bytes 375022848 | solution.py:233
  433.6 12.2 fusion.127
  456.5 22.8 %multiply_convert_fusion.7 = (bf16[8192,512]{0,1:T(8,128)(2,1)}, bf16[8192,512]{0,1:T(8,128)(2,1)}, bf16[8192,512]{0,1:T(8,128)(2,1)}) fusion(f32[8192,1024]{0,1:T(8,128)} %fusion.127, bf16[512,128]{1,0:T(8,128)(2,1)S(1)} %get-tuple-element.560, f32[8192,128]{1,0:T(8,128)} %fusion.124), kind=kOutput, calls=%fused_computation.3.clone.1 | convolution fusion | flops 1137704960 | bytes 63045632 | tf_op jit(solution)/shard_map/while/body/eval_jaxpr/dot_general | solution.py:25
  479.3 13.2 %fusion.128 = (f32[8192]{0:T(1024)S(1)}, f32[8192]{0:T(1024)S(1)}, f32[8192,128]{1,0:T(8,128)S(1)}) fusion(f32[8192]{0:T(1024)S(1)} %add_rsqrt_fusion.3, f32[8192,128]{1,0:T(8,128)S(1)} %copy-done.2, f32[8192]{0:T(1024)S(1)} %broadcast_multiply_fusion.13, bf16[128,1024]{1,0:T(8,128)(2,1)S(1)} %copy-done.10, ...), kind=kOutput, calls=%fused_computation.108.clone.1 | convolution fusion | flops 2186264576 | bytes 25559040 | tf_op jit(solution)/shard_map/while/body/eval_jaxpr/dot_general | solution.py:25
  492.5 5.0 bitcast_reduce_fusion.2
  500.7 11.2 fusion.130
  511.9 7.8 convolution_add_fusion.7
  519.7 12.6 %fusion.129 = f32[128,1024]{1,0:T(8,128)S(1)} fusion(bf16[8192,512]{0,1:T(8,128)(2,1)} %get-tuple-element.491, bf16[8192,512]{0,1:T(8,128)(2,1)} %get-tuple-element.492, f32[128,1024]{1,0:T(8,128)S(1)} %copy-done.25, pred[]{:T(512)S(6)} %compare.3, f32[8192,128]{1,0:T(8,128)S(1)} %copy-done.3, f32[8192]{0:T(1024)S(1)} %add_rsqrt_fusion.3, ...), kind=kOutput, calls=%fused_computation.23.clone.1 | convolution fusion | flops 2184445952 | bytes 22085632 | tf_op jit(solution)/shard_map/while/body/eval_jaxpr/dot_general | solution.py:19
  550.1 12.2 fusion.127
  573.0 22.8 %multiply_convert_fusion.7 = (bf16[8192,512]{0,1:T(8,128)(2,1)}, bf16[8192,512]{0,1:T(8,128)(2,1)}, bf16[8192,512]{0,1:T(8,128)(2,1)}) fusion(f32[8192,1024]{0,1:T(8,128)} %fusion.127, bf16[512,128]{1,0:T(8,128)(2,1)S(1)} %get-tuple-element.560, f32[8192,128]{1,0:T(8,128)} %fusion.124), kind=kOutput, calls=%fused_computation.3.clone.1 | convolution fusion | flops 1137704960 | bytes 63045632 | tf_op jit(solution)/shard_map/while/body/eval_jaxpr/dot_general | solution.py:25
  595.8 13.2 %fusion.128 = (f32[8192]{0:T(1024)S(1)}, f32[8192]{0:T(1024)S(1)}, f32[8192,128]{1,0:T(8,128)S(1)}) fusion(f32[8192]{0:T(1024)S(1)} %add_rsqrt_fusion.3, f32[8192,128]{1,0:T(8,128)S(1)} %copy-done.2, f32[8192]{0:T(1024)S(1)} %broadcast_multiply_fusion.13, bf16[128,1024]{1,0:T(8,128)(2,1)S(1)} %copy-done.10, ...), kind=kOutput, calls=%fused_computation.108.clone.1 | convolution fusion | flops 2186264576 | bytes 25559040 | tf_op jit(solution)/shard_map/while/body/eval_jaxpr/dot_general | solution.py:25
  609.0 5.0 bitcast_reduce_fusion.2
  617.2 11.2 fusion.130
  628.4 7.8 convolution_add_fusion.7
  636.2 12.6 %fusion.129 = f32[128,1024]{1,0:T(8,128)S(1)} fusion(bf16[8192,512]{0,1:T(8,128)(2,1)} %get-tuple-element.491, bf16[8192,512]{0,1:T(8,128)(2,1)} %get-tuple-element.492, f32[128,1024]{1,0:T(8,128)S(1)} %copy-done.25, pred[]{:T(512)S(6)} %compare.3, f32[8192,128]{1,0:T(8,128)S(1)} %copy-done.3, f32[8192]{0:T(1024)S(1)} %add_rsqrt_fusion.3, ...), kind=kOutput, calls=%fused_computation.23.clone.1 | convolution fusion | flops 2184445952 | bytes 22085632 | tf_op jit(solution)/shard_map/while/body/eval_jaxpr/dot_general | solution.py:19
  666.6 12.2 fusion.127
  689.5 22.8 %multiply_convert_fusion.7 = (bf16[8192,512]{0,1:T(8,128)(2,1)}, bf16[8192,512]{0,1:T(8,128)(2,1)}, bf16[8192,512]{0,1:T(8,128)(2,1)}) fusion(f32[8192,1024]{0,1:T(8,128)} %fusion.127, bf16[512,128]{1,0:T(8,128)(2,1)S(1)} %get-tuple-element.560, f32[8192,128]{1,0:T(8,128)} %fusion.124), kind=kOutput, calls=%fused_computation.3.clone.1 | convolution fusion | flops 1137704960 | bytes 63045632 | tf_op jit(solution)/shard_map/while/body/eval_jaxpr/dot_general | solution.py:25
  712.2 13.2 %fusion.128 = (f32[8192]{0:T(1024)S(1)}, f32[8192]{0:T(1024)S(1)}, f32[8192,128]{1,0:T(8,128)S(1)}) fusion(f32[8192]{0:T(1024)S(1)} %add_rsqrt_fusion.3, f32[8192,128]{1,0:T(8,128)S(1)} %copy-done.2, f32[8192]{0:T(1024)S(1)} %broadcast_multiply_fusion.13, bf16[128,1024]{1,0:T(8,128)(2,1)S(1)} %copy-done.10, ...), kind=kOutput, calls=%fused_computation.108.clone.1 | convolution fusion | flops 2186264576 | bytes 25559040 | tf_op jit(solution)/shard_map/while/body/eval_jaxpr/dot_general | solution.py:25
  725.5 5.0 bitcast_reduce_fusion.2
  733.6 11.2 fusion.130
  744.9 7.8 convolution_add_fusion.7
  752.7 12.6 %fusion.129 = f32[128,1024]{1,0:T(8,128)S(1)} fusion(bf16[8192,512]{0,1:T(8,128)(2,1)} %get-tuple-element.491, bf16[8192,512]{0,1:T(8,128)(2,1)} %get-tuple-element.492, f32[128,1024]{1,0:T(8,128)S(1)} %copy-done.25, pred[]{:T(512)S(6)} %compare.3, f32[8192,128]{1,0:T(8,128)S(1)} %copy-done.3, f32[8192]{0:T(1024)S(1)} %add_rsqrt_fusion.3, ...), kind=kOutput, calls=%fused_computation.23.clone.1 | convolution fusion | flops 2184445952 | bytes 22085632 | tf_op jit(solution)/shard_map/while/body/eval_jaxpr/dot_general | solution.py:19
  783.1 12.2 fusion.127
  806.0 22.8 %multiply_convert_fusion.7 = (bf16[8192,512]{0,1:T(8,128)(2,1)}, bf16[8192,512]{0,1:T(8,128)(2,1)}, bf16[8192,512]{0,1:T(8,128)(2,1)}) fusion(f32[8192,1024]{0,1:T(8,128)} %fusion.127, bf16[512,128]{1,0:T(8,128)(2,1)S(1)} %get-tuple-element.560, f32[8192,128]{1,0:T(8,128)} %fusion.124), kind=kOutput, calls=%fused_computation.3.clone.1 | convolution fusion | flops 1137704960 | bytes 63045632 | tf_op jit(solution)/shard_map/while/body/eval_jaxpr/dot_general | solution.py:25
  828.7 13.2 %fusion.128 = (f32[8192]{0:T(1024)S(1)}, f32[8192]{0:T(1024)S(1)}, f32[8192,128]{1,0:T(8,128)S(1)}) fusion(f32[8192]{0:T(1024)S(1)} %add_rsqrt_fusion.3, f32[8192,128]{1,0:T(8,128)S(1)} %copy-done.2, f32[8192]{0:T(1024)S(1)} %broadcast_multiply_fusion.13, bf16[128,1024]{1,0:T(8,128)(2,1)S(1)} %copy-done.10, ...), kind=kOutput, calls=%fused_computation.108.clone.1 | convolution fusion | flops 2186264576 | bytes 25559040 | tf_op jit(solution)/shard_map/while/body/eval_jaxpr/dot_general | solution.py:25
  842.0 5.0 bitcast_reduce_fusion.2
  850.1 11.2 fusion.130
  861.4 7.8 convolution_add_fusion.7
  869.2 12.6 %fusion.129 = f32[128,1024]{1,0:T(8,128)S(1)} fusion(bf16[8192,512]{0,1:T(8,128)(2,1)} %get-tuple-element.491, bf16[8192,512]{0,1:T(8,128)(2,1)} %get-tuple-element.492, f32[128,1024]{1,0:T(8,128)S(1)} %copy-done.25, pred[]{:T(512)S(6)} %compare.3, f32[8192,128]{1,0:T(8,128)S(1)} %copy-done.3, f32[8192]{0:T(1024)S(1)} %add_rsqrt_fusion.3, ...), kind=kOutput, calls=%fused_computation.23.clone.1 | convolution fusion | flops 2184445952 | bytes 22085632 | tf_op jit(solution)/shard_map/while/body/eval_jaxpr/dot_general | solution.py:19
  890.3 14.0 %psum.98 = bf16[128,128]{1,0:T(8,128)(2,1)S(1)} all-reduce(bf16[128,128]{1,0:T(8,128)(2,1)S(1)} %convert_element_type.121), channel_id=1, replica_groups=mesh['row'=4,'col'=8] {'row'}, use_global_device_ids=true, to_apply=%region_10.11 | all-reduce | flops 16384 | bytes 65536 | tf_op jit(solution)/shard_map/psum | solution.py:241
  904.3 14.2 %all_gather.11 = bf16[1024,128]{1,0:T(8,128)(2,1)S(1)} all-gather(bf16[128,128]{1,0:T(8,128)(2,1)S(1)} %psum.98), channel_id=1, replica_groups=mesh['row'=4,'col'=8] {'col'}, dimensions={0}, use_global_device_ids=true | all-gather | bytes 294912 | tf_op jit(solution)/shard_map/all_gather | solution.py:242
  920.2 26.6 %reduce-scatter.2.cloned.1.call-done = bf16[32,128]{1,0:T(8,128)(2,1)} async-done(((bf16[256,128]{1,0:T(8,128)(2,1)}), bf16[32,128]{1,0:T(8,128)(2,1)}) %reduce-scatter.2.cloned.1.call-update) | async-done | bytes 8208 | tf_op jit(solution)/shard_map/reduce_scatter | solution.py:238
  955.1 50.2 %all-reduce.10.cloned.1.call-done = (f32[128,1024]{1,0:T(8,128)}, f32[512,128]{1,0:T(8,128)}, f32[128,128]{1,0:T(8,128)}, f32[384,128]{1,0:T(8,128)}, f32[384,128]{1,0:T(8,128)}) async-done(((f32[128,1024]{1,0:T(8,128)}, f32[512,128]{1,0:T(8,128)}, f32[128,128]{1,0:T(8,128)}, f32[384,128]{1,0:T(8,128)}, f32[384,128]{1,0:T(8,128)}), (f32[128,1024]{1,0:T(8,128)}, f32[512,128]{1,0:T(8,128)}, ...) | async-done | bytes 1245200 | tf_op jit(solution)/shard_map/psum | solution.py:257
  1012.5 15.7 %psum.105 = f32[65,128]{1,0:T(8,128)S(1)} all-reduce(f32[65,128]{1,0:T(8,128)S(1)} %copy-done.20), channel_id=1, replica_groups=mesh['row'=4,'col'=8] {'row'}, use_global_device_ids=true, to_apply=%region_18.19 | all-reduce | flops 8320 | bytes 66560 | tf_op jit(solution)/shard_map/psum | solution.py:257
  1028.3 26.6 %psum.106 = f32[65,128]{1,0:T(8,128)S(1)} all-reduce(f32[65,128]{1,0:T(8,128)S(1)} %psum.105), channel_id=1, replica_groups=mesh['row'=4,'col'=8] {'col'}, use_global_device_ids=true, to_apply=%region_19.20 | all-reduce | flops 8320 | bytes 66560 | tf_op jit(solution)/shard_map/psum | solution.py:256
  1057.3 11.6 all-reduce.8.cloned.1.call-done
  1075.7 162.3 %all-reduce.6.cloned.1.call-done = f32[3,384,1536]{2,1,0:T(8,128)} async-done(((f32[3,384,1536]{2,1,0:T(8,128)}), f32[3,384,1536]{2,1,0:T(8,128)}) %all-reduce.6.cloned.1.call-update) | async-done | bytes 7077904 | tf_op jit(solution)/shard_map/psum | solution.py:253
  (327 shorter events, 168.9 us)
Async XLA Ops:
  7.2 255.1 %copy-start = (bf16[384,1536]{1,0:T(8,128)(2,1)S(1)}, bf16[384,1536]{1,0:T(8,128)(2,1)}, u32[]{:S(2)}) copy-start(bf16[384,1536]{1,0:T(8,128)(2,1)} %param.30) | copy-start | bytes 3538948
  254.2 7.6 copy-start.16
  254.2 7.7 copy-start.11
  254.2 146.6 %all-to-all-start.2 = ((bf16[8,128,2048]{2,1,0:T(8,128)(2,1)}), bf16[8,128,2048]{2,1,0:T(8,128)(2,1)}, u32[]{:S(2)}, u32[]{:S(2)}) async-start(bf16[8,128,2048]{2,1,0:T(8,128)(2,1)} %bitcast.135), calls=%async_computation.2 | async-start | bytes 8388608 | tf_op jit(solution)/shard_map/all_to_all | solution.py:187
  258.9 101.1 %copy-start.34 = (bf16[384,128]{1,0:T(8,128)(2,1)S(1)}, bf16[384,128]{1,0:T(8,128)(2,1)}, u32[]{:S(2)}) copy-start(bf16[384,128]{1,0:T(8,128)(2,1)} %param.28) | copy-start | bytes 294916
  258.9 141.2 %copy-start.35 = (bf16[128,512]{1,0:T(8,128)(2,1)S(1)}, bf16[128,512]{1,0:T(8,128)(2,1)}, u32[]{:S(2)}) copy-start(bf16[128,512]{1,0:T(8,128)(2,1)} %param.23) | copy-start | bytes 393220
  258.9 141.2 %copy-start.36 = (bf16[128,512]{1,0:T(8,128)(2,1)S(1)}, bf16[128,512]{1,0:T(8,128)(2,1)}, u32[]{:S(2)}) copy-start(bf16[128,512]{1,0:T(8,128)(2,1)} %param.22) | copy-start | bytes 393220
  258.9 687.9 %reduce-scatter.2.cloned.1.call-start = ((), (), s32[]{:S(2)}) async-start(), calls=%async_computation.4 | async-start | bytes 73728 | tf_op jit(solution)/shard_map/reduce_scatter | solution.py:238
  262.3 137.8 %copy-start.23 = (f32[32,1536]{1,0:T(8,128)}, f32[32,1536]{1,0:T(8,128)S(1)}, u32[]{:S(2)}) copy-start(f32[32,1536]{1,0:T(8,128)S(1)} %fusion.52) | copy-start | bytes 589828
  263.3 96.8 %copy-start.21 = (bf16[32,1536]{1,0:T(8,128)(2,1)}, bf16[32,1536]{1,0:T(8,128)(2,1)S(1)}, u32[]{:S(2)}) copy-start(bf16[32,1536]{1,0:T(8,128)(2,1)S(1)} %get-tuple-element.354) | copy-start | bytes 294916
  264.9 135.1 %copy-start.24 = (bf16[32,384]{1,0:T(8,128)(2,1)}, bf16[32,384]{1,0:T(8,128)(2,1)S(1)}, u32[]{:S(2)}) copy-start(bf16[32,384]{1,0:T(8,128)(2,1)S(1)} %fusion.26) | copy-start | bytes 73732
  425.8 27.4 %copy-start.6 = (bf16[1,64,128,128]{3,2,1,0:T(8,128)(2,1)}, bf16[1,64,128,128]{3,2,1,0:T(8,128)(2,1)S(1)}, u32[]{:S(2)}) copy-start(bf16[1,64,128,128]{3,2,1,0:T(8,128)(2,1)S(1)} %get-tuple-element.487) | copy-start | bytes 6291460 | tf_op jit(solution)/shard_map/while
  431.1 14.7 %copy-start.1 = (f32[8192,128]{1,0:T(8,128)}, f32[8192,128]{1,0:T(8,128)S(1)}, u32[]{:S(2)}) copy-start(f32[8192,128]{1,0:T(8,128)S(1)} %get-tuple-element.489) | copy-start | bytes 12582916 | tf_op jit(solution)/shard_map/while
  456.5 22.8 %copy-start.2 = (f32[8192,128]{1,0:T(8,128)S(1)}, f32[8192,128]{1,0:T(8,128)}, u32[]{:S(2)}) copy-start(f32[8192,128]{1,0:T(8,128)} %copy-done.1) | copy-start | bytes 12582916 | tf_op jit(solution)/shard_map/while
  456.5 22.8 %copy-start.10 = (bf16[128,1024]{1,0:T(8,128)(2,1)S(1)}, bf16[128,1024]{1,0:T(8,128)(2,1)}, u32[]{:S(2)}) copy-start(bf16[128,1024]{1,0:T(8,128)(2,1)} %get-tuple-element.561) | copy-start | bytes 786436 | tf_op jit(solution)/shard_map/while
  479.3 13.3 %copy-start.5 = (f32[8192,128]{1,0:T(8,128)S(1)}, f32[8192,128]{1,0:T(8,128)}, u32[]{:S(2)}) copy-start(f32[8192,128]{1,0:T(8,128)} %fusion.124) | copy-start | bytes 12582916 | tf_op jit(solution)/shard_map/while
  511.9 7.8 copy-start.3
  511.9 7.8 copy-start.25
  542.3 27.4 %copy-start.6 = (bf16[1,64,128,128]{3,2,1,0:T(8,128)(2,1)}, bf16[1,64,128,128]{3,2,1,0:T(8,128)(2,1)S(1)}, u32[]{:S(2)}) copy-start(bf16[1,64,128,128]{3,2,1,0:T(8,128)(2,1)S(1)} %get-tuple-element.487) | copy-start | bytes 6291460 | tf_op jit(solution)/shard_map/while
  547.6 14.7 %copy-start.1 = (f32[8192,128]{1,0:T(8,128)}, f32[8192,128]{1,0:T(8,128)S(1)}, u32[]{:S(2)}) copy-start(f32[8192,128]{1,0:T(8,128)S(1)} %get-tuple-element.489) | copy-start | bytes 12582916 | tf_op jit(solution)/shard_map/while
  573.0 22.8 %copy-start.2 = (f32[8192,128]{1,0:T(8,128)S(1)}, f32[8192,128]{1,0:T(8,128)}, u32[]{:S(2)}) copy-start(f32[8192,128]{1,0:T(8,128)} %copy-done.1) | copy-start | bytes 12582916 | tf_op jit(solution)/shard_map/while
  573.0 22.8 %copy-start.10 = (bf16[128,1024]{1,0:T(8,128)(2,1)S(1)}, bf16[128,1024]{1,0:T(8,128)(2,1)}, u32[]{:S(2)}) copy-start(bf16[128,1024]{1,0:T(8,128)(2,1)} %get-tuple-element.561) | copy-start | bytes 786436 | tf_op jit(solution)/shard_map/while
  595.7 13.3 %copy-start.5 = (f32[8192,128]{1,0:T(8,128)S(1)}, f32[8192,128]{1,0:T(8,128)}, u32[]{:S(2)}) copy-start(f32[8192,128]{1,0:T(8,128)} %fusion.124) | copy-start | bytes 12582916 | tf_op jit(solution)/shard_map/while
  628.4 7.8 copy-start.3
  628.4 7.8 copy-start.25
  658.8 27.4 %copy-start.6 = (bf16[1,64,128,128]{3,2,1,0:T(8,128)(2,1)}, bf16[1,64,128,128]{3,2,1,0:T(8,128)(2,1)S(1)}, u32[]{:S(2)}) copy-start(bf16[1,64,128,128]{3,2,1,0:T(8,128)(2,1)S(1)} %get-tuple-element.487) | copy-start | bytes 6291460 | tf_op jit(solution)/shard_map/while
  664.1 14.7 %copy-start.1 = (f32[8192,128]{1,0:T(8,128)}, f32[8192,128]{1,0:T(8,128)S(1)}, u32[]{:S(2)}) copy-start(f32[8192,128]{1,0:T(8,128)S(1)} %get-tuple-element.489) | copy-start | bytes 12582916 | tf_op jit(solution)/shard_map/while
  689.5 22.8 %copy-start.2 = (f32[8192,128]{1,0:T(8,128)S(1)}, f32[8192,128]{1,0:T(8,128)}, u32[]{:S(2)}) copy-start(f32[8192,128]{1,0:T(8,128)} %copy-done.1) | copy-start | bytes 12582916 | tf_op jit(solution)/shard_map/while
  689.5 22.8 %copy-start.10 = (bf16[128,1024]{1,0:T(8,128)(2,1)S(1)}, bf16[128,1024]{1,0:T(8,128)(2,1)}, u32[]{:S(2)}) copy-start(bf16[128,1024]{1,0:T(8,128)(2,1)} %get-tuple-element.561) | copy-start | bytes 786436 | tf_op jit(solution)/shard_map/while
  712.2 13.3 %copy-start.5 = (f32[8192,128]{1,0:T(8,128)S(1)}, f32[8192,128]{1,0:T(8,128)}, u32[]{:S(2)}) copy-start(f32[8192,128]{1,0:T(8,128)} %fusion.124) | copy-start | bytes 12582916 | tf_op jit(solution)/shard_map/while
  744.9 7.8 copy-start.3
  744.9 7.8 copy-start.25
  775.3 27.4 %copy-start.6 = (bf16[1,64,128,128]{3,2,1,0:T(8,128)(2,1)}, bf16[1,64,128,128]{3,2,1,0:T(8,128)(2,1)S(1)}, u32[]{:S(2)}) copy-start(bf16[1,64,128,128]{3,2,1,0:T(8,128)(2,1)S(1)} %get-tuple-element.487) | copy-start | bytes 6291460 | tf_op jit(solution)/shard_map/while
  780.6 14.7 %copy-start.1 = (f32[8192,128]{1,0:T(8,128)}, f32[8192,128]{1,0:T(8,128)S(1)}, u32[]{:S(2)}) copy-start(f32[8192,128]{1,0:T(8,128)S(1)} %get-tuple-element.489) | copy-start | bytes 12582916 | tf_op jit(solution)/shard_map/while
  806.0 22.8 %copy-start.2 = (f32[8192,128]{1,0:T(8,128)S(1)}, f32[8192,128]{1,0:T(8,128)}, u32[]{:S(2)}) copy-start(f32[8192,128]{1,0:T(8,128)} %copy-done.1) | copy-start | bytes 12582916 | tf_op jit(solution)/shard_map/while
  806.0 22.8 %copy-start.10 = (bf16[128,1024]{1,0:T(8,128)(2,1)S(1)}, bf16[128,1024]{1,0:T(8,128)(2,1)}, u32[]{:S(2)}) copy-start(bf16[128,1024]{1,0:T(8,128)(2,1)} %get-tuple-element.561) | copy-start | bytes 786436 | tf_op jit(solution)/shard_map/while
  828.7 13.3 %copy-start.5 = (f32[8192,128]{1,0:T(8,128)S(1)}, f32[8192,128]{1,0:T(8,128)}, u32[]{:S(2)}) copy-start(f32[8192,128]{1,0:T(8,128)} %fusion.124) | copy-start | bytes 12582916 | tf_op jit(solution)/shard_map/while
  861.4 7.8 copy-start.3
  861.4 7.8 copy-start.25
  889.5 64.3 %copy-start.38 = (f32[32]{0:T(128)S(1)}, f32[32]{0:T(128)}, u32[]{:S(2)}) copy-start(f32[32]{0:T(128)} %copy-done.37) | copy-start | bytes 388
  918.5 86.7 %all-reduce.10.cloned.1.call-start = ((), (), s32[]{:S(2)}) async-start(), calls=%async_computation.7 | async-start | bytes 2490368 | tf_op jit(solution)/shard_map/psum | solution.py:257
  948.4 120.5 %all-reduce.8.cloned.1.call-start = ((), (), s32[]{:S(2)}) async-start(), calls=%async_computation.6 | async-start | bytes 2490368 | tf_op jit(solution)/shard_map/psum | solution.py:256
  1005.3 232.7 %all-reduce.6.cloned.1.call-start = ((), (), s32[]{:S(2)}) async-start(), calls=%async_computation.5 | async-start | bytes 14155776 | tf_op jit(solution)/shard_map/psum | solution.py:253
  1011.8 43.7 %copy-start.12 = (bf16[384,1536]{1,0:T(8,128)(2,1)S(1)}, bf16[384,1536]{1,0:T(8,128)(2,1)}, u32[]{:S(2)}) copy-start(bf16[384,1536]{1,0:T(8,128)(2,1)} %param.29) | copy-start | bytes 3538948
  1011.8 43.7 %copy-start.32 = (bf16[32,1536]{1,0:T(8,128)(2,1)S(1)}, bf16[32,1536]{1,0:T(8,128)(2,1)}, u32[]{:S(2)}) copy-start(bf16[32,1536]{1,0:T(8,128)(2,1)} %get-tuple-element.353) | copy-start | bytes 294916
  1011.8 44.2 %copy-start.17 = (bf16[32,384]{1,0:T(8,128)(2,1)S(1)}, bf16[32,384]{1,0:T(8,128)(2,1)}, u32[]{:S(2)}) copy-start(bf16[32,384]{1,0:T(8,128)(2,1)} %param.20) | copy-start | bytes 73732
  1011.8 44.2 %copy-start.31 = (bf16[32,1536]{1,0:T(8,128)(2,1)S(1)}, bf16[32,1536]{1,0:T(8,128)(2,1)}, u32[]{:S(2)}) copy-start(bf16[32,1536]{1,0:T(8,128)(2,1)} %copy-done.30) | copy-start | bytes 294916
  1011.8 44.8 %copy-start.29 = (f32[32,384]{1,0:T(8,128)S(1)}, f32[32,384]{1,0:T(8,128)}, u32[]{:S(2)}) copy-start(f32[32,384]{1,0:T(8,128)} %copy-done.28) | copy-start | bytes 147460
  (50 other events, 148.1 us)
Sparse Core Ops, SparseCore 0:
  918.6 28.1 reduce-scatter.1
  951.5 53.6 all-reduce.9
  1008.0 60.8 all-reduce.7
  1074.6 163.4 all-reduce.5
